TPU v7x, 32 devices: a whole 2x2x4 slice. The times are simulated.
32 devices in a mesh: land: 8 (over y, x, core), sea: 4 (over z).
Axes of the slice: x: 2, y: 2, z: 4, core: 2. Of those that a mesh axis runs over, the one named last changes fastest.
Arguments:
- adj_depth: float32 [4096, 2048], P('land', 'sea'), may hold values from -6 to 6
- conductance: float32 [4096, 2048], P('land', 'sea'), may hold values from 0.02 to 0.24
- wet: int32 [4, 4096, 2048], P(None, 'land', 'sea'), may hold values 0 or 1
- coast_cell: int32 [262144], P(('land', 'sea')), may hold values from 0 to 262143
- coast_dest: int32 [262144, 1], P(('land', 'sea')), may hold values from 0 to 31; in each aligned block of 8192 rows (0 to 8191, 8192 to 16383, ...) at most 512 rows name the same one
- coast_node: int32 [262144], P(('land', 'sea')), may hold values from 0 to 16383
- coast_weight: float32 [262144], P(('land', 'sea')), may hold values from 0.2 to 2
- adj_ocean: float32 [4096, 128], P(('land', 'sea')), may hold values from -6 to 6
- ocean_blocks: bfloat16 [4096, 2, 128, 128], P(('land', 'sea')), may hold values from -0.375 to 0.375
- ocean_target: int32 [4096, 2], P(('land', 'sea')), may hold values from 0 to 511
Outputs:
- land_out: float32 [4096, 2048], P('land', 'sea')
- ocean_out: float32 [4096, 128], P(('land', 'sea'))
Inputs may be any that keep to these rules, and one draw needn't show every extreme that they name: `coast_dest`: in each device's 8192 rows no partition is named by more than 512 entries, and one is named by exactly 512. `ocean_target`: blocks are numbered within the group of the 4 devices that share a land index.
All inputs are finite; a program needn't handle non-finite values. No bound on the sum of `wet` on one device may be relied on, other than what follows from the above.
Results may differ from a plain program's by a relative error of at most 0.0036.
Values sent between devices are 32-bit elements; how exact they have to be, the bound alone decides.
A program may use at most 128 MiB of HBM per device.

v0:
```python
import jax
import jax.numpy as jnp
from jax import lax
from jax.sharding import PartitionSpec as P

STEPS = 4


def extended(block, sides, width):
    for axis, dim in sides:
        count = lax.axis_size(axis)
        forward = [(i, i + 1) for i in range(count - 1)]
        backward = [(target, source) for source, target in forward]
        low = lax.ppermute(
            lax.slice_in_dim(block, block.shape[dim] - width, None, axis=dim), axis, forward
        )
        high = lax.ppermute(lax.slice_in_dim(block, 0, width, axis=dim), axis, backward)
        block = jnp.concatenate([low, block, high], axis=dim)
    return block


def send_coast(value_send, node_send):
    got_values, got_nodes = (
        lax.all_to_all(value_send, ("land", "sea"), split_axis=0, concat_axis=0, tiled=True),
        lax.all_to_all(node_send, ("land", "sea"), split_axis=0, concat_axis=0, tiled=True),
    )
    return (got_values, got_nodes)


def local(
    adj_depth,
    conductance,
    wet,
    coast_cell,
    coast_dest,
    coast_node,
    coast_weight,
    adj_ocean,
    ocean_blocks,
    ocean_target,
):
    devices = lax.axis_size(("land", "sea"))
    group = lax.axis_size("sea")
    blocks, depth = ocean_target.shape
    width = adj_ocean.shape[1]
    cells = adj_depth.shape[0] * adj_depth.shape[1]
    capacity = 2 * coast_cell.shape[0] // devices
    destination = coast_dest[:, 0]
    matches = (destination[:, None] == jnp.arange(devices, dtype=jnp.int32)[None, :]).astype(
        jnp.int32
    )
    running = jnp.cumsum(matches, axis=0)
    slot_index = jnp.take_along_axis(running, destination[:, None], axis=1)[:, 0] - 1
    flat_slot = destination * capacity + slot_index
    node_send = jnp.zeros((devices * capacity,), jnp.int32).at[flat_slot].set(coast_node)
    node_send = node_send.reshape(devices, 1, capacity)
    slot_cell = jnp.full((devices * capacity,), cells, jnp.int32).at[flat_slot].set(coast_cell)
    slot_weight = jnp.zeros((devices * capacity,), jnp.float32).at[flat_slot].set(coast_weight)
    target_flat = ocean_target.reshape(-1)
    owned_first = lax.axis_index("sea") * blocks
    block_ids = jnp.arange(blocks, dtype=jnp.int32)
    lane_ids = jnp.arange(width, dtype=jnp.int32)
    land_adj = adj_depth
    ocean_adj = adj_ocean
    for timestep in range(STEPS):
        wet_now = wet[timestep].astype(jnp.float32)
        masked = jnp.concatenate([(wet_now * land_adj).reshape(-1), jnp.zeros((1,), jnp.float32)])
        value_send = (
            (slot_weight * jnp.take(masked, slot_cell))
            .reshape(devices, capacity)
            .reshape(devices, 1, capacity)
        )
        got_values, got_nodes = send_coast(value_send, node_send)
        ocean_got_values = got_values[:, 0, :]
        node_flat = got_nodes.reshape(-1)
        value_flat = ocean_got_values.reshape(-1)
        block_hot = (node_flat[:, None] // width == block_ids[None, :]).astype(jnp.float32)
        lane_hot = jnp.where(
            node_flat[:, None] % width == lane_ids[None, :], value_flat[:, None], 0.0
        )
        coupled = jnp.einsum("eb,ew->bw", block_hot, lane_hot, precision=lax.Precision.HIGHEST)
        ocean_low = ocean_adj.astype(jnp.bfloat16)
        terms = jnp.einsum(
            "bkij,bi->bkj", ocean_blocks, ocean_low, preferred_element_type=jnp.float32
        ).reshape(-1, width)
        marker = (
            target_flat[:, None] == jnp.arange(blocks * group, dtype=jnp.int32)[None, :]
        ).astype(jnp.float32)
        summed = jnp.einsum("rc,rw->cw", marker, terms, precision=lax.Precision.HIGHEST)
        summed = lax.psum(summed, "sea")
        owned = lax.dynamic_slice_in_dim(summed, owned_first, blocks, 0)
        ocean_adj = 0.5 * ocean_adj + owned + coupled
        spread = conductance * wet_now * land_adj
        padded = extended(spread, (("land", 0), ("sea", 1)), 1)
        beside_all = padded[2:, 1:-1] + padded[:-2, 1:-1] + padded[1:-1, 2:] + padded[1:-1, :-2]
        land_adj = land_adj + (beside_all - 4.0 * spread)
    return (land_adj, ocean_adj)


def solution(mesh):
    in_specs = (
        P("land", "sea"),
        P("land", "sea"),
        P(None, "land", "sea"),
        P(("land", "sea")),
        P(("land", "sea"), None),
        P(("land", "sea")),
        P(("land", "sea")),
        P(("land", "sea"), None),
        P(("land", "sea"), None, None, None),
        P(("land", "sea"), None),
    )
    out_specs = (P("land", "sea"), P(("land", "sea"), None))
    return jax.shard_map(local, mesh=mesh, in_specs=in_specs, out_specs=out_specs, check_vma=False)
```

profile of v0, /device:TPU:0, one launch (start us, length us, event | category | flops | bytes accessed | tf_op | source)
XLA Modules:
  0.0 834.4 jit_solution(16540205699284803208)
XLA Ops:
  14.9 9.5 %reduce-window.6 = s32[32,64,128]{2,1,0:T(8,128)S(1)} reduce-window(s32[32,64,128]{2,1,0:T(8,128)S(1)} %fusion.64, s32[]{:T(128)} %constant.83.clone.1), window={size=1x1x128 pad=0_0x0_0x127_0}, to_apply=%region_1.2 | reduce-window | flops 33292288 | bytes 2097156 | tf_op jit(solution)/shard_map/reduce-window
  26.7 65.5 %gather_fusion = s32[8192]{0:T(1024)S(1)} fusion(s32[8192,32]{0,1:T(8,128)S(1)} %bitcast.102, s32[8192]{0:T(1024)S(1)} %bitcast.103), kind=kCustom, calls=%fused_computation.4 | custom fusion | bytes 131072 | tf_op jit(solution)/shard_map/jit(take_along_axis)/gather | solution.py:53
  92.4 31.2 %scatter_custom_fusion = s32[16384]{0:T(1024)} fusion(s32[8192]{0:T(1024)S(1)} %bitcast.120, s32[8192]{0:T(1024)} %param.17, s32[]{:T(128)} %constant.83.clone.1), kind=kCustom, calls=%fused_computation.175 | custom fusion | bytes 66048 | tf_op jit(solution)/shard_map/scatter | solution.py:55
  123.6 8.0 all-to-all-start
  133.3 5.3 collective-permute-start.3
  154.2 30.6 %scatter_custom_fusion.2 = s32[16384]{0:T(1024)S(1)} fusion(s32[8192]{0:T(1024)} %bitcast.121, s32[8192]{0:T(1024)} %param.15, s32[]{:T(128)} %constant.95.clone.1), kind=kCustom, calls=%fused_computation.171 | custom fusion | bytes 66048 | tf_op jit(solution)/shard_map/scatter | solution.py:57
  187.0 5.9 collective-permute-start.7
  195.4 30.8 %scatter_custom_fusion.1 = f32[16384]{0:T(1024)S(1)} fusion(s32[8192]{0:T(1024)} %bitcast.122, f32[8192]{0:T(1024)} %param.18, f32[]{:T(128)} %constant.93.clone.1), kind=kCustom, calls=%fused_computation.173 | custom fusion | bytes 66048 | tf_op jit(solution)/shard_map/scatter | solution.py:58
  237.9 90.5 %gather_fusion.1 = f32[16384]{0:T(1024)S(1)} fusion(f32[262145]{0:T(1024)S(1)} %get-tuple-element.37, s32[16384]{0:T(1024)S(1)} %fusion.82), kind=kCustom, calls=%fused_computation.clone | custom fusion | bytes 196608 | tf_op jit(solution)/shard_map/jit(_take)/gather | solution.py:69
  331.7 5.3 collective-permute-start.11
  337.6 90.5 %gather_fusion.2 = f32[16384]{0:T(1024)S(1)} fusion(f32[262145]{0:T(1024)S(1)} %get-tuple-element.36, s32[16384]{0:T(1024)S(1)} %fusion.82), kind=kCustom, calls=%fused_computation.1.clone | custom fusion | bytes 196608 | tf_op jit(solution)/shard_map/jit(_take)/gather | solution.py:69
  439.3 90.5 %gather_fusion.3 = f32[16384]{0:T(1024)S(1)} fusion(f32[262145]{0:T(1024)S(1)} %get-tuple-element.35, s32[16384]{0:T(1024)S(1)} %fusion.82), kind=kCustom, calls=%fused_computation.2.clone | custom fusion | bytes 196608 | tf_op jit(solution)/shard_map/jit(_take)/gather | solution.py:69
  529.8 90.5 %gather_fusion.4 = f32[16384]{0:T(1024)S(1)} fusion(f32[262145]{0:T(1024)S(1)} %get-tuple-element.34, s32[16384]{0:T(1024)S(1)} %fusion.82), kind=kCustom, calls=%fused_computation.3.clone | custom fusion | bytes 196608 | tf_op jit(solution)/shard_map/jit(_take)/gather | solution.py:69
  634.4 6.7 all-to-all-start.1
  651.7 12.0 %fusion.24 = f32[128,128]{1,0:T(8,128)S(1)} fusion(f32[16384]{0:T(1024)S(1)} %bitcast.119, s32[16384]{0:T(1024)S(1)} %get-tuple-element.33, f32[512,128]{1,0:T(8,128)} %all-reduce.5.cloned.1.call-done, s32[]{:T(128)S(6)} %select_n.73, f32[128,128]{1,0:T(8,128)S(1)} %copy-done.9, pred[16384,128]{1,0:T(32,128)(4,1)S(1)} %iota_compare_fusion.27), kind=kOutput, calls=%fused_computation.38 | convolution fusion | flops 3225468928 | bytes 2424836 | tf_op jit(solution)/shard_map/eb,ew->bw/dot_general | solution.py:81
  663.7 4.6 fusion.77
  672.7 5.8 all-to-all-start.3
  678.6 28.7 %all-reduce.7.cloned.1.call-done = f32[512,128]{1,0:T(8,128)} async-done(((f32[512,128]{1,0:T(8,128)}), f32[512,128]{1,0:T(8,128)}) %all-reduce.7.cloned.1.call-update) | async-done | bytes 262160 | tf_op jit(solution)/shard_map/psum | solution.py:90
  707.3 12.0 %fusion.27 = f32[128,128]{1,0:T(8,128)S(1)} fusion(f32[16384]{0:T(1024)S(1)} %bitcast.117, s32[16384]{0:T(1024)S(1)} %get-tuple-element.33, f32[512,128]{1,0:T(8,128)} %all-reduce.7.cloned.1.call-done, s32[]{:T(128)S(6)} %select_n.73, f32[128,128]{1,0:T(8,128)S(1)} %fusion.24, pred[16384,128]{1,0:T(32,128)(4,1)S(1)} %iota_compare_fusion.28), kind=kOutput, calls=%fused_computation.39 | convolution fusion | flops 3225468928 | bytes 2424836 | tf_op jit(solution)/shard_map/eb,ew->bw/dot_general | solution.py:81
  719.3 4.6 fusion.75
  732.9 28.8 %all-reduce.9.cloned.1.call-done = f32[512,128]{1,0:T(8,128)} async-done(((f32[512,128]{1,0:T(8,128)}), f32[512,128]{1,0:T(8,128)}) %all-reduce.9.cloned.1.call-update) | async-done | bytes 262160 | tf_op jit(solution)/shard_map/psum | solution.py:90
  761.7 12.0 %fusion.30 = f32[128,128]{1,0:T(8,128)S(1)} fusion(f32[16384]{0:T(1024)S(1)} %bitcast.116, s32[16384]{0:T(1024)S(1)} %get-tuple-element.33, f32[512,128]{1,0:T(8,128)} %all-reduce.9.cloned.1.call-done, s32[]{:T(128)S(6)} %select_n.73, f32[128,128]{1,0:T(8,128)S(1)} %fusion.27, pred[16384,128]{1,0:T(32,128)(4,1)S(1)} %iota_compare_fusion.29), kind=kOutput, calls=%fused_computation.40 | convolution fusion | flops 3225468928 | bytes 2424836 | tf_op jit(solution)/shard_map/eb,ew->bw/dot_general | solution.py:81
  782.6 32.4 %all-reduce.11.cloned.1.call-done = f32[512,128]{1,0:T(8,128)} async-done(((f32[512,128]{1,0:T(8,128)}), f32[512,128]{1,0:T(8,128)}) %all-reduce.11.cloned.1.call-update) | async-done | bytes 262160 | tf_op jit(solution)/shard_map/psum | solution.py:90
  815.0 12.6 %fusion.33 = f32[128,128]{1,0:T(8,128)} fusion(f32[16384]{0:T(1024)S(1)} %bitcast.118, s32[16384]{0:T(1024)S(1)} %get-tuple-element.33, f32[512,128]{1,0:T(8,128)} %all-reduce.11.cloned.1.call-done, s32[]{:T(128)S(6)} %select_n.73, f32[128,128]{1,0:T(8,128)S(1)} %fusion.30, pred[16384,128]{1,0:T(32,128)(4,1)S(1)} %iota_compare_fusion.30), kind=kOutput, calls=%fused_computation.41 | convolution fusion | flops 3225468928 | bytes 2424836 | tf_op jit(solution)/shard_map/eb,ew->bw/dot_general | solution.py:81
  (121 shorter events, 105.3 us)
Async XLA Ops:
  10.4 121.4 %collective-permute-start = (f32[1,512]{1,0:T(1,128)S(1)}, f32[1,512]{1,0:T(1,128)S(1)}, u32[]{:S(2)}, u32[]{:S(2)}) collective-permute-start(f32[1,512]{1,0:T(1,128)S(1)} %get-tuple-element.28), channel_id=1, source_target_pairs={{4,0},{8,4},{12,8},{16,12},{20,16},{24,20},{28,24},{5,1},{9,5},{13... | collective-permute-start | bytes 6152 | tf_op jit(solution)/shard_map/ppermute | solution.py:17
  11.7 120.1 %collective-permute-start.1 = (f32[1,512]{1,0:T(1,128)S(1)}, f32[1,512]{1,0:T(1,128)S(1)}, u32[]{:S(2)}, u32[]{:S(2)}) collective-permute-start(f32[1,512]{1,0:T(1,128)S(1)} %get-tuple-element.27), channel_id=1, source_target_pairs={{0,4},{4,8},{8,12},{12,16},{16,20},{20,24},{24,28},{1,5},{5,9},{9,... | collective-permute-start | bytes 6152 | tf_op jit(solution)/shard_map/ppermute | solution.py:14
  123.6 510.8 %all-to-all-start = ((s32[32,1,512]{2,1,0:T(1,128)}), s32[32,1,512]{2,1,0:T(1,128)}, u32[]{:S(2)}, u32[]{:S(2)}) async-start(s32[32,1,512]{2,1,0:T(1,128)} %bitcast.15), calls=%async_computation | async-start | bytes 131072 | tf_op jit(solution)/shard_map/all_to_all | solution.py:25
  131.7 519.9 %all-reduce.5.cloned.1.call-start = ((), (), s32[]{:S(2)}) async-start(), calls=%async_computation.5 | async-start | bytes 524288 | tf_op jit(solution)/shard_map/psum | solution.py:90
  131.9 11.4 %collective-permute-start.2 = (f32[514,1]{1,0:T(8,128)S(1)}, f32[514,1]{1,0:T(8,128)S(1)}, u32[]{:S(2)}, u32[]{:S(2)}) collective-permute-start(f32[514,1]{1,0:T(8,128)S(1)} %get-tuple-element.19), channel_id=1, source_target_pairs={{1,0},{2,1},{3,2},{5,4},{6,5},{7,6},{9,8},{10,9},{11,10},{13,12},{... | collective-permute-start | bytes 6176 | tf_op jit(solution)/shard_map/ppermute | solution.py:17
  148.4 36.4 %collective-permute-start.4 = (f32[1,512]{1,0:T(1,128)S(1)}, f32[1,512]{1,0:T(1,128)S(1)}, u32[]{:S(2)}, u32[]{:S(2)}) collective-permute-start(f32[1,512]{1,0:T(1,128)S(1)} %get-tuple-element.26), channel_id=1, source_target_pairs={{4,0},{8,4},{12,8},{16,12},{20,16},{24,20},{28,24},{5,1},{9,5},{13... | collective-permute-start | bytes 6152 | tf_op jit(solution)/shard_map/ppermute | solution.py:17
  149.7 35.1 %collective-permute-start.5 = (f32[1,512]{1,0:T(1,128)S(1)}, f32[1,512]{1,0:T(1,128)S(1)}, u32[]{:S(2)}, u32[]{:S(2)}) collective-permute-start(f32[1,512]{1,0:T(1,128)S(1)} %get-tuple-element.25), channel_id=1, source_target_pairs={{0,4},{4,8},{8,12},{12,16},{16,20},{20,24},{24,28},{1,5},{5,9},{9,... | collective-permute-start | bytes 6152 | tf_op jit(solution)/shard_map/ppermute | solution.py:14
  185.7 42.0 %collective-permute-start.6 = (f32[514,1]{1,0:T(8,128)}, f32[514,1]{1,0:T(8,128)}, u32[]{:S(2)}, u32[]{:S(2)}) collective-permute-start(f32[514,1]{1,0:T(8,128)} %get-tuple-element.17), channel_id=1, source_target_pairs={{1,0},{2,1},{3,2},{5,4},{6,5},{7,6},{9,8},{10,9},{11,10},{13,12},{... | collective-permute-start | bytes 6176 | tf_op jit(solution)/shard_map/ppermute | solution.py:17
  187.0 40.7 %collective-permute-start.7 = (f32[514,1]{1,0:T(8,128)}, f32[514,1]{1,0:T(8,128)}, u32[]{:S(2)}, u32[]{:S(2)}) collective-permute-start(f32[514,1]{1,0:T(8,128)} %get-tuple-element.18), channel_id=1, source_target_pairs={{0,1},{1,2},{2,3},{4,5},{5,6},{6,7},{8,9},{9,10},{10,11},{12,13},{... | collective-permute-start | bytes 6176 | tf_op jit(solution)/shard_map/ppermute | solution.py:14
  232.9 95.6 %collective-permute-start.8 = (f32[1,512]{1,0:T(1,128)S(1)}, f32[1,512]{1,0:T(1,128)S(1)}, u32[]{:S(2)}, u32[]{:S(2)}) collective-permute-start(f32[1,512]{1,0:T(1,128)S(1)} %get-tuple-element.24), channel_id=1, source_target_pairs={{4,0},{8,4},{12,8},{16,12},{20,16},{24,20},{28,24},{5,1},{9,5},{13... | collective-permute-start | bytes 6152 | tf_op jit(solution)/shard_map/ppermute | solution.py:17
  234.2 94.3 %collective-permute-start.9 = (f32[1,512]{1,0:T(1,128)S(1)}, f32[1,512]{1,0:T(1,128)S(1)}, u32[]{:S(2)}, u32[]{:S(2)}) collective-permute-start(f32[1,512]{1,0:T(1,128)S(1)} %get-tuple-element.23), channel_id=1, source_target_pairs={{0,4},{4,8},{8,12},{12,16},{16,20},{20,24},{24,28},{1,5},{5,9},{9,... | collective-permute-start | bytes 6152 | tf_op jit(solution)/shard_map/ppermute | solution.py:14
  330.4 99.2 %collective-permute-start.10 = (f32[514,1]{1,0:T(8,128)}, f32[514,1]{1,0:T(8,128)}, u32[]{:S(2)}, u32[]{:S(2)}) collective-permute-start(f32[514,1]{1,0:T(8,128)} %get-tuple-element.15), channel_id=1, source_target_pairs={{1,0},{2,1},{3,2},{5,4},{6,5},{7,6},{9,8},{10,9},{11,10},{13,12},{... | collective-permute-start | bytes 6176 | tf_op jit(solution)/shard_map/ppermute | solution.py:17
  331.7 98.0 %collective-permute-start.11 = (f32[514,1]{1,0:T(8,128)}, f32[514,1]{1,0:T(8,128)}, u32[]{:S(2)}, u32[]{:S(2)}) collective-permute-start(f32[514,1]{1,0:T(8,128)} %get-tuple-element.16), channel_id=1, source_target_pairs={{0,1},{1,2},{2,3},{4,5},{5,6},{6,7},{8,9},{9,10},{10,11},{12,13},{... | collective-permute-start | bytes 6176 | tf_op jit(solution)/shard_map/ppermute | solution.py:14
  434.1 186.3 %collective-permute-start.12 = (f32[1,512]{1,0:T(1,128)S(1)}, f32[1,512]{1,0:T(1,128)S(1)}, u32[]{:S(2)}, u32[]{:S(2)}) collective-permute-start(f32[1,512]{1,0:T(1,128)S(1)} %get-tuple-element.22), channel_id=1, source_target_pairs={{4,0},{8,4},{12,8},{16,12},{20,16},{24,20},{28,24},{5,1},{9,5},{13... | collective-permute-start | bytes 6152 | tf_op jit(solution)/shard_map/ppermute | solution.py:17
  435.4 185.0 %collective-permute-start.13 = (f32[1,512]{1,0:T(1,128)S(1)}, f32[1,512]{1,0:T(1,128)S(1)}, u32[]{:S(2)}, u32[]{:S(2)}) collective-permute-start(f32[1,512]{1,0:T(1,128)S(1)} %get-tuple-element.21), channel_id=1, source_target_pairs={{0,4},{4,8},{8,12},{12,16},{16,20},{20,24},{24,28},{1,5},{5,9},{9,... | collective-permute-start | bytes 6152 | tf_op jit(solution)/shard_map/ppermute | solution.py:14
  620.5 10.4 %collective-permute-start.14 = (f32[514,1]{1,0:T(8,128)S(1)}, f32[514,1]{1,0:T(8,128)S(1)}, u32[]{:S(2)}, u32[]{:S(2)}) collective-permute-start(f32[514,1]{1,0:T(8,128)S(1)} %get-tuple-element.13), channel_id=1, source_target_pairs={{1,0},{2,1},{3,2},{5,4},{6,5},{7,6},{9,8},{10,9},{11,10},{13,12},{... | collective-permute-start | bytes 6176 | tf_op jit(solution)/shard_map/ppermute | solution.py:17
  621.8 10.9 %collective-permute-start.15 = (f32[514,1]{1,0:T(8,128)S(1)}, f32[514,1]{1,0:T(8,128)S(1)}, u32[]{:S(2)}, u32[]{:S(2)}) collective-permute-start(f32[514,1]{1,0:T(8,128)S(1)} %get-tuple-element.14), channel_id=1, source_target_pairs={{0,1},{1,2},{2,3},{4,5},{5,6},{6,7},{8,9},{9,10},{10,11},{12,13},{... | collective-permute-start | bytes 6176 | tf_op jit(solution)/shard_map/ppermute | solution.py:14
  634.4 14.2 %all-to-all-start.1 = ((f32[32,1,512]{2,1,0:T(1,128)}), f32[32,1,512]{2,1,0:T(1,128)S(1)}, u32[]{:S(2)}, u32[]{:S(2)}) async-start(f32[32,1,512]{2,1,0:T(1,128)} %bitcast.17), calls=%async_computation.1 | async-start | bytes 131072 | tf_op jit(solution)/shard_map/all_to_all | solution.py:24
  648.6 24.0 %all-to-all-start.2 = ((f32[32,1,512]{2,1,0:T(1,128)}), f32[32,1,512]{2,1,0:T(1,128)S(1)}, u32[]{:S(2)}, u32[]{:S(2)}) async-start(f32[32,1,512]{2,1,0:T(1,128)} %bitcast.23), calls=%async_computation.2 | async-start | bytes 131072 | tf_op jit(solution)/shard_map/all_to_all | solution.py:24
  651.2 56.1 %all-reduce.7.cloned.1.call-start = ((), (), s32[]{:S(2)}) async-start(), calls=%async_computation.6 | async-start | bytes 524288 | tf_op jit(solution)/shard_map/psum | solution.py:90
  672.7 55.8 %all-to-all-start.3 = ((f32[32,1,512]{2,1,0:T(1,128)}), f32[32,1,512]{2,1,0:T(1,128)S(1)}, u32[]{:S(2)}, u32[]{:S(2)}) async-start(f32[32,1,512]{2,1,0:T(1,128)} %bitcast.29), calls=%async_computation.3 | async-start | bytes 131072 | tf_op jit(solution)/shard_map/all_to_all | solution.py:24
  678.5 83.2 %all-reduce.9.cloned.1.call-start = ((), (), s32[]{:S(2)}) async-start(), calls=%async_computation.7 | async-start | bytes 524288 | tf_op jit(solution)/shard_map/psum | solution.py:90
  728.5 54.1 %all-to-all-start.4 = ((f32[32,1,512]{2,1,0:T(1,128)}), f32[32,1,512]{2,1,0:T(1,128)S(1)}, u32[]{:S(2)}, u32[]{:S(2)}) async-start(f32[32,1,512]{2,1,0:T(1,128)} %bitcast.35), calls=%async_computation.4 | async-start | bytes 131072 | tf_op jit(solution)/shard_map/all_to_all | solution.py:24
  732.9 82.2 %all-reduce.11.cloned.1.call-start = ((), (), s32[]{:S(2)}) async-start(), calls=%async_computation.8 | async-start | bytes 524288 | tf_op jit(solution)/shard_map/psum | solution.py:90
  (13 other events, 430.8 us)
Sparse Core Ops, SparseCore 0:
  154.3 37.5 all-reduce.4
  670.0 37.2 all-reduce.6
  725.8 35.7 all-reduce.8
  779.9 35.0 all-reduce.10
where the time goes:
time: 844 us; the launch traced here: 834 us
  local copies, waits for them, and re-layouts  528 us (63%)
  waiting for transfers between devices  99.6 us (12%)
  matrix products  73.2 us (9%)
  starting transfers between devices  72.6 us (9%)
  other arithmetic  46.3 us (5%)
  between operations  14.7 us (2%)
    gather x4, local copies, waits for them, and re-layouts, local(): jnp.take(masked, slot_cell)  362 us
    psum x4, waiting for transfers between devices, local(): summed = lax.psum(summed, 'sea')  89.9 us
    gather x1, local copies, waits for them, and re-layouts, local(): jnp.take_along_axis(running, destination[:, None], axis=1)[:, 0] - 1  65.5 us
    dot_general x4, matrix products, local(): jnp.einsum('eb,ew->bw', block_hot, lane_hot, precision=lax.Precision.HIGH...  48.5 us
    ppermute x8, starting transfers between devices, extended(): lax.ppermute(lax.slice_in_dim(block, block.shape[dim] - width, None, axis...  34.2 us
    scatter x1, local copies, waits for them, and re-layouts, local(): jnp.zeros((devices * capacity,), jnp.int32).at[flat_slot].set(coast_node)  31.2 us
    scatter x1, local copies, waits for them, and re-layouts, local(): jnp.zeros((devices * capacity,), jnp.float32).at[flat_slot]  30.8 us
    scatter x1, local copies, waits for them, and re-layouts, local(): jnp.full((devices * capacity,), cells, jnp.int32).at[flat_slot]  30.6 us
  transfers between devices with their start and end apart: 25, of which 7 were waited for; matrix products, arithmetic and copies ran while one was open for 76% of the time, Pallas kernels for 0%

commit v1 on v0

v1 whole, which is shorter than its diff:
```python
import functools

import jax
import jax.numpy as jnp
from jax import lax
from jax.experimental import pallas as pl
from jax.experimental.pallas import tpu as pltpu
from jax.sharding import PartitionSpec as P

STEPS = 4
LANES = 128
SUB = 8
HALO = STEPS


def exchanged(last, first, axis):
    count = lax.axis_size(axis)
    forward = [(i, i + 1) for i in range(count - 1)]
    backward = [(target, source) for source, target in forward]
    return lax.ppermute(last, axis, forward), lax.ppermute(first, axis, backward)


def fields(depth, conductance, wet, rows, columns):
    return jnp.concatenate(
        [
            depth[None, rows, columns],
            conductance[None, rows, columns],
            wet[:, rows, columns].astype(jnp.float32),
        ],
        axis=0,
    )


def land_kernel(depth, cond, wet, left, right, top, bottom, out, masked, ext):
    rows, cols = depth.shape
    mid_r, mid_c = pl.ds(SUB, rows), pl.ds(LANES, cols)
    ext[0, mid_r, mid_c] = depth[...]
    ext[1, mid_r, mid_c] = cond[...]
    for t in range(STEPS):
        ext[2 + t, mid_r, mid_c] = wet[t].astype(jnp.float32)
    for i in range(2 + STEPS):
        ext[i, mid_r, pl.ds(0, LANES)] = left[i]
        ext[i, mid_r, pl.ds(LANES + cols, LANES)] = right[i]
        ext[i, pl.ds(0, SUB), :] = top[i]
        ext[i, pl.ds(SUB + rows, SUB), :] = bottom[i]
    height, width = ext.shape[1], ext.shape[2]
    for t in range(STEPS):
        wet_land = ext[2 + t] * ext[0]
        masked[t] = wet_land[SUB : SUB + rows, LANES : LANES + cols].astype(jnp.bfloat16)
        spread = ext[1] * wet_land
        beside = (
            pltpu.roll(spread, 1, 0)
            + pltpu.roll(spread, height - 1, 0)
            + pltpu.roll(spread, 1, 1)
            + pltpu.roll(spread, width - 1, 1)
        )
        ext[0] = ext[0] + (beside - 4.0 * spread)
    out[...] = ext[0, mid_r, mid_c]


def land_steps(depth, cond, wet):
    rows, cols = depth.shape
    every = slice(None)
    pick = functools.partial(fields, depth, cond, wet)
    first_c = pick(every, slice(0, HALO))
    last_c = pick(every, slice(cols - HALO, cols))
    left, right = exchanged(
        last_c.transpose(0, 2, 1), first_c.transpose(0, 2, 1), "sea"
    )
    left, right = left.transpose(0, 2, 1), right.transpose(0, 2, 1)

    def wide(where):
        return jnp.concatenate(
            [left[:, where], pick(where, every), right[:, where]], axis=2
        )

    top, bottom = exchanged(
        wide(slice(rows - HALO, rows)), wide(slice(0, HALO)), "land"
    )
    side = LANES - HALO
    left = jnp.pad(left, ((0, 0), (0, 0), (side, 0)))
    right = jnp.pad(right, ((0, 0), (0, 0), (0, side)))
    top = jnp.pad(top, ((0, 0), (SUB - HALO, 0), (side, side)))
    bottom = jnp.pad(bottom, ((0, 0), (0, SUB - HALO), (side, side)))
    return pl.pallas_call(
        land_kernel,
        out_shape=(
            jax.ShapeDtypeStruct((rows, cols), jnp.float32),
            jax.ShapeDtypeStruct((STEPS, rows, cols), jnp.bfloat16),
        ),
        scratch_shapes=[
            pltpu.VMEM((2 + STEPS, rows + 2 * SUB, cols + 2 * LANES), jnp.float32)
        ],
        compiler_params=pltpu.CompilerParams(vmem_limit_bytes=48 << 20),
        name="land_steps",
    )(depth, cond, wet, left, right, top, bottom)


def iota(shape, axis):
    return lax.broadcasted_iota(jnp.int32, shape, axis)


def halves(value):
    high = value.astype(jnp.bfloat16).astype(jnp.float32)
    return high, value - high


def across(a, b):
    return lax.dot_general(
        a, b, (((1,), (1,)), ((), ())), preferred_element_type=jnp.float32
    )


def placed(row, lane, values, rows):
    count = row.shape[1]
    row_hot = jnp.where(iota((rows, count), 0) == row, 1.0, 0.0).astype(jnp.bfloat16)
    lane_is = iota((LANES, count), 0) == lane
    spreads = [jnp.where(lane_is, v, 0.0).astype(jnp.bfloat16) for v in values]
    return across(row_hot, jnp.concatenate(spreads, axis=0))


def send_kernel(capacity, piece, cell, dest, node, weight, masked, out, acc, carry):
    step = pl.program_id(0)
    devices = carry.shape[0]
    cols = masked.shape[2]
    count = cell.shape[2]

    @pl.when(step == 0)
    def _():
        acc[...] = jnp.zeros_like(acc)
        carry[...] = jnp.zeros_like(carry)

    dest_now = dest[0]
    matches = jnp.where(iota((devices, count), 0) == dest_now, 1.0, 0.0)
    triangle = jnp.where(
        iota((piece, piece), 0) <= iota((piece, piece), 1), 1.0, 0.0
    ).astype(jnp.bfloat16)
    base = carry[:, 0:1]
    ranks = []
    for p in range(count // piece):
        own = matches[:, p * piece : (p + 1) * piece]
        running = jnp.dot(
            own.astype(jnp.bfloat16), triangle, preferred_element_type=jnp.float32
        )
        ranks.append(jnp.sum(own * (running + base), axis=0, keepdims=True))
        base = base + jnp.sum(own, axis=1, keepdims=True)
    carry[...] = jnp.broadcast_to(base, carry.shape)
    rank = jnp.concatenate(ranks, axis=1).astype(jnp.int32) - 1
    slot = dest_now * capacity + rank

    place = cell[0]
    cell_row, cell_col = place // cols, place % cols
    col_hot = jnp.where(iota((cols, count), 0) == cell_col, 1.0, 0.0).astype(jnp.bfloat16)
    row_is = iota((masked.shape[1], count), 0) == cell_row
    values = []
    for t in range(STEPS):
        lines = jnp.dot(masked[t], col_hot, preferred_element_type=jnp.float32)
        found = jnp.sum(jnp.where(row_is, lines, 0.0), axis=0, keepdims=True)
        values.extend(halves(weight[0] * found))
    node_now = node[0]
    values.append((node_now // LANES).astype(jnp.float32))
    values.append((node_now % LANES).astype(jnp.float32))
    acc[...] += placed(slot // LANES, slot % LANES, values, acc.shape[0])

    @pl.when(step == pl.num_programs(0) - 1)
    def _():
        def block(i):
            return acc[:, i * LANES : (i + 1) * LANES]

        for t in range(STEPS):
            out[t] = block(2 * t) + block(2 * t + 1)
        out[STEPS] = block(2 * STEPS) * float(LANES) + block(2 * STEPS + 1)


def packed(masked, cell, dest, node, weight, devices):
    entries = cell.shape[0]
    count = 1024
    steps = entries // count
    capacity = 2 * entries // devices
    rows = devices * capacity // LANES
    line = pl.BlockSpec((1, 1, count), lambda i: (i, 0, 0))
    shape = (steps, 1, count)
    return pl.pallas_call(
        functools.partial(send_kernel, capacity, 256),
        grid=(steps,),
        in_specs=[line] * 4 + [pl.BlockSpec(masked.shape, lambda i: (0, 0, 0))],
        out_specs=pl.BlockSpec((STEPS + 1, rows, LANES), lambda i: (0, 0, 0)),
        out_shape=jax.ShapeDtypeStruct((STEPS + 1, rows, LANES), jnp.float32),
        scratch_shapes=[
            pltpu.VMEM((rows, (2 * STEPS + 2) * LANES), jnp.float32),
            pltpu.VMEM((devices, LANES), jnp.float32),
        ],
        compiler_params=pltpu.CompilerParams(vmem_limit_bytes=48 << 20),
        name="coast_pack",
    )(cell.reshape(shape), dest.reshape(shape), node.reshape(shape), weight.reshape(shape), masked)


def couple_kernel(got, out, acc):
    step = pl.program_id(0)

    @pl.when(step == 0)
    def _():
        acc[...] = jnp.zeros_like(acc)

    node = got[STEPS : STEPS + 1, :].astype(jnp.int32)
    values = []
    for t in range(STEPS):
        values.extend(halves(got[t : t + 1, :]))
    acc[...] += placed(node // LANES, node % LANES, values, acc.shape[0])

    @pl.when(step == pl.num_programs(0) - 1)
    def _():
        for t in range(STEPS):
            at = 2 * t * LANES
            out[t] = acc[:, at : at + LANES] + acc[:, at + LANES : at + 2 * LANES]


def coupled_steps(got, blocks):
    slots = got.shape[1]
    count = 2048
    return pl.pallas_call(
        couple_kernel,
        grid=(slots // count,),
        in_specs=[pl.BlockSpec((STEPS + 1, count), lambda i: (0, i))],
        out_specs=pl.BlockSpec((STEPS, blocks, LANES), lambda i: (0, 0, 0)),
        out_shape=jax.ShapeDtypeStruct((STEPS, blocks, LANES), jnp.float32),
        scratch_shapes=[pltpu.VMEM((blocks, 2 * STEPS * LANES), jnp.float32)],
        compiler_params=pltpu.CompilerParams(vmem_limit_bytes=48 << 20),
        name="coast_couple",
    )(got)


def local(
    adj_depth,
    conductance,
    wet,
    coast_cell,
    coast_dest,
    coast_node,
    coast_weight,
    adj_ocean,
    ocean_blocks,
    ocean_target,
):
    devices = lax.axis_size(("land", "sea"))
    group = lax.axis_size("sea")
    blocks = ocean_target.shape[0]
    width = adj_ocean.shape[1]
    land_out, masked = land_steps(adj_depth, conductance, wet)
    packs = packed(masked, coast_cell, coast_dest, coast_node, coast_weight, devices)
    packs = packs.reshape(STEPS + 1, devices, -1).transpose(1, 0, 2)
    got = lax.all_to_all(packs, ("land", "sea"), split_axis=0, concat_axis=0, tiled=True)
    coupled = coupled_steps(got.transpose(1, 0, 2).reshape(STEPS + 1, -1), blocks)

    target_flat = ocean_target.reshape(-1)
    marker = (
        target_flat[:, None] == jnp.arange(blocks * group, dtype=jnp.int32)[None, :]
    ).astype(jnp.float32)
    ocean_adj = adj_ocean
    for timestep in range(STEPS):
        ocean_low = ocean_adj.astype(jnp.bfloat16)
        terms = jnp.einsum(
            "bkij,bi->bkj", ocean_blocks, ocean_low, preferred_element_type=jnp.float32
        ).reshape(-1, width)
        summed = jnp.einsum("rc,rw->cw", marker, terms, precision=lax.Precision.HIGHEST)
        parts = lax.all_to_all(
            summed.reshape(group, blocks, width), "sea", split_axis=0, concat_axis=0, tiled=True
        )
        ocean_adj = 0.5 * ocean_adj + jnp.sum(parts, axis=0) + coupled[timestep]
    return (land_out, ocean_adj)


def solution(mesh):
    in_specs = (
        P("land", "sea"),
        P("land", "sea"),
        P(None, "land", "sea"),
        P(("land", "sea")),
        P(("land", "sea"), None),
        P(("land", "sea")),
        P(("land", "sea")),
        P(("land", "sea"), None),
        P(("land", "sea"), None, None, None),
        P(("land", "sea"), None),
    )
    out_specs = (P("land", "sea"), P(("land", "sea"), None))
    return jax.shard_map(local, mesh=mesh, in_specs=in_specs, out_specs=out_specs, check_vma=False)
```

time: 844 us -> 169 us (0.20); the launches traced: 834 us -> 168 us
  local copies, waits for them, and re-layouts: 528 us -> 23.3 us
  waiting for transfers between devices: 99.6 us -> 14.4 us
  matrix products: 73.2 us -> 20.7 us
  starting transfers between devices: 72.6 us -> 22.7 us
  Pallas kernels: 0 us -> 48.4 us
  other arithmetic: 46.3 us -> 2.56 us
  blocking collectives: 0 us -> 34.8 us
  between operations: 14.7 us -> 0.95 us
    gather x5 -> x0, local copies, waits for them, and re-layouts: 428 us -> none  [the longest x4 362 us: local(): jnp.take(masked, slot_cell)]
    scatter x3 -> x0, local copies, waits for them, and re-layouts: 92.7 us -> none  [the longest x1 31.2 us: local(): jnp.zeros((devices * capacity,), jnp.int32).at[flat_slot].set(coast_node)]
    psum x4 -> x0, waiting for transfers between devices: 89.9 us -> none  [local(): summed = lax.psum(summed, 'sea')]
    dot_general x4 -> x0, matrix products: 48.5 us -> none  [local(): jnp.einsum('eb,ew->bw', block_hot, lane_hot, precision=lax.Precision.HIGH...]
    pallas_call x0 -> x3, Pallas kernels: none -> 48.4 us  [the longest x1 28.1 us: packed(): pl.pallas_call(functools.partial(send_kernel, capacity, 256), grid=(steps...]
    all_to_all x0 -> x3, blocking collectives: none -> 34.8 us  [local(): lax.all_to_all(summed.reshape(group, blocks, width), 'sea', split_axis=0,...]
    ppermute x16 -> x4, starting transfers between devices: 44.5 us -> 10.7 us  [the longest x2 8.13 us: exchanged(): lax.ppermute(last, axis, forward)]
    all_to_all x5 -> x2, starting transfers between devices: 27.5 us -> 12 us  [the longest x1 6.06 us: local(): lax.all_to_all(packs, ('land', 'sea'), split_axis=0, concat_axis=0, tiled...]
  transfers between devices with their start and end apart: 25 -> 6, of which waited for: 7 -> 1; matrix products, arithmetic and copies ran while one was open for 76% -> 11% of each run, Pallas kernels for 0% -> 22%
where the time goes in v1:
time: 169 us; the launch traced here: 168 us
  Pallas kernels  48.4 us (29%)
  blocking collectives  34.8 us (21%)
  local copies, waits for them, and re-layouts  23.3 us (14%)
  starting transfers between devices  22.7 us (13%)
  matrix products  20.7 us (12%)
  waiting for transfers between devices  14.4 us (9%)
  other arithmetic  2.56 us (2%)
    all_to_all x3, blocking collectives, local(): lax.all_to_all(summed.reshape(group, blocks, width), 'sea', split_axis=0,...  34.8 us
    pallas_call x1, Pallas kernels, packed(): pl.pallas_call(functools.partial(send_kernel, capacity, 256), grid=(steps...  28.1 us
    dot_general x4, matrix products, local(): jnp.einsum('bkij,bi->bkj', ocean_blocks, ocean_low, preferred_element_typ...  18.3 us
    all_to_all x1, waiting for transfers between devices, local(): lax.all_to_all(packs, ('land', 'sea'), split_axis=0, concat_axis=0, tiled...  14.3 us
    pallas_call x1, Pallas kernels, coupled_steps(): pl.pallas_call(couple_kernel, grid=(slots // count,), in_specs=[pl.BlockS...  12.2 us
    ppermute x2, starting transfers between devices, exchanged(): lax.ppermute(last, axis, forward)  8.13 us
    pallas_call x1, Pallas kernels, land_steps(): pl.pallas_call(land_kernel, out_shape=(jax.ShapeDtypeStruct((rows, cols),...  8.07 us
    unnamed x23, local copies, waits for them, and re-layouts  7.73 us
  transfers between devices with their start and end apart: 6, of which 1 were waited for; matrix products, arithmetic and copies ran while one was open for 11% of the time, Pallas kernels for 22%

profile of v1, /device:TPU:0, one launch (start us, length us, event | category | flops | bytes accessed | tf_op | source)
XLA Modules:
  0.0 167.8 jit_solution(9382289600801422044)
XLA Ops:
  0.6 2.9 %fusion.29 = (s32[4,512,4]{2,1,0:T(8,128)S(1)}, s32[4,512,4]{2,1,0:T(8,128)}) fusion(s32[4,512,512]{2,1,0:T(8,128)} %wet.1), kind=kLoop, calls=%fused_computation.48 | loop fusion | bytes 131072 | tf_op jit(solution)/shard_map/slice | solution.py:28
  3.5 1.7 %copy.33 = s32[4,512,4]{1,2,0:T(4,128)S(1)} copy(s32[4,512,4]{2,1,0:T(8,128)} %get-tuple-element.11) | data formatting | bytes 65536
  5.3 1.9 %fusion.32 = (f32[512,4]{1,0:T(8,128)S(1)}, f32[512,4]{1,0:T(8,128)}) fusion(f32[512,512]{1,0:T(8,128)} %depth.1), kind=kLoop, calls=%fused_computation.51 | loop fusion | bytes 32768 | tf_op jit(solution)/shard_map/slice | solution.py:26
  8.2 1.9 %fusion.33 = (f32[512,4]{1,0:T(8,128)}, f32[512,4]{1,0:T(8,128)}) fusion(f32[512,512]{1,0:T(8,128)} %cond.1), kind=kLoop, calls=%fused_computation.52 | loop fusion | bytes 32768 | tf_op jit(solution)/shard_map/slice | solution.py:27
  11.8 4.9 %collective-permute-start = (f32[6,4,512]{2,1,0:T(4,128)}, f32[6,4,512]{2,1,0:T(4,128)S(1)}, u32[]{:S(2)}, u32[]{:S(2)}) collective-permute-start(f32[6,4,512]{2,1,0:T(4,128)} %maximum_bitcast_fusion), channel_id=1, source_target_pairs={{0,1},{1,2},{2,3},{4,5},{5,6},{6,7},{8,9},{9,10},{10,11},{12,13},{... | collective-permute-start | bytes 147464 | tf_op jit(solution)/shard_map/ppermute | solution.py:20
  20.6 4.6 %fusion.26 = f32[128,1,2,128]{3,1,2,0:T(1,128)S(1)} fusion(bf16[128,2,128,128]{3,2,1,0:T(8,128)(2,1)} %param.18, bf16[128,128,1,1]{1,0,2,3:T(8,128)(2,1)S(1)} %convert_bitcast_fusion.3), kind=kOutput, calls=%fused_computation.31 | convolution fusion | flops 8388608 | bytes 8552448 | tf_op jit(solution)/shard_map/bkij,bi->bkj/dot_general | solution.py:262
  26.3 5.9 %all-to-all-start = ((f32[4,128,128]{2,1,0:T(8,128)}), f32[4,128,128]{2,1,0:T(8,128)S(1)}, u32[]{:S(2)}, u32[]{:S(2)}) async-start(f32[4,128,128]{2,1,0:T(8,128)} %fusion.6), calls=%async_computation | async-start | bytes 524288 | tf_op jit(solution)/shard_map/all_to_all | solution.py:266
  33.1 1.7 %copy.16 = f32[6,4,512]{1,2,0:T(8,128)} copy(f32[6,4,512]{2,1,0:T(4,128)S(1)} %collective-permute-done) | data formatting | bytes 98304 | tf_op jit(solution)/shard_map/ppermute | solution.py:20
  34.8 1.7 copy.20
  38.8 3.2 %collective-permute-start.2 = (f32[6,4,520]{2,1,0:T(4,128)S(1)}, f32[6,4,520]{2,1,0:T(4,128)S(1)}, u32[]{:S(2)}, u32[]{:S(2)}) collective-permute-start(f32[6,4,520]{2,1,0:T(4,128)S(1)} %pad_maximum_fusion), channel_id=1, source_target_pairs={{0,4},{4,8},{8,12},{12,16},{16,20},{20,24},{24,28},{1,5},{5,9},{9,... | collective-permute-start | bytes 149768 | tf_op jit(solution)/shard_map/ppermute | solution.py:20
  42.1 1.9 %pad.16.left = f32[6,512,128]{2,1,0:T(8,128)S(1)} pad(f32[6,512,4]{2,1,0:T(8,128)} %bitcast.100, f32[]{:T(128)} %constant.2.clone.1), padding=0_0x0_0x124_0 | pad | bytes 1622020 | tf_op jit(solution)/shard_map/jit(_pad)/pad | solution.py:81
  44.0 1.5 pad.17.right
  45.7 8.1 %land_steps.1 = (f32[512,512]{1,0:T(8,128)}, bf16[4,512,512]{2,1,0:T(8,128)(2,1)}) custom-call(f32[512,512]{1,0:T(8,128)S(1)} %copy-done, f32[512,512]{1,0:T(8,128)S(1)} %copy-done.1, s32[4,512,512]{2,1,0:T(8,128)} %wet.1, f32[6,512,128]{2,1,0:T(8,128)S(1)} %pad.16.left, f32[6,512,128]{2,1,0:T(8,128)S(1)} %pad.17.right, f32[6,8,768]{2,1,0:T(8,128)S(1)} %pad.18.top, ...), custom_call_target="tpu_custom_call" | custom-call | tf_op jit(solution)/shard_map/land_steps/pallas_call | solution.py:85
  53.8 1.6 copy-done.2
  55.4 28.1 %coast_pack.1 = f32[5,128,128]{2,1,0:T(8,128)S(1)} custom-call(s32[8,1,1024]{2,1,0:T(1,128)S(1)} %bitcast.95, s32[8,1,1024]{2,1,0:T(1,128)S(1)} %bitcast.96, s32[8,1,1024]{2,1,0:T(1,128)S(1)} %bitcast.97, f32[8,1,1024]{2,1,0:T(1,128)S(1)} %bitcast.98, bf16[4,512,512]{2,1,0:T(8,128)(2,1)S(1)} %copy-done.2), custom_call_target="tpu_custom_call" | custom-call | tf_op jit(solution)/shard_map/coast_pack/pallas_call | solution.py:183
  84.6 6.1 %all-to-all-start.1 = ((f32[32,5,512]{2,1,0:T(8,128)}), f32[32,5,512]{2,1,0:T(8,128)S(1)}, u32[]{:S(2)}, u32[]{:S(2)}) async-start(f32[32,5,512]{2,1,0:T(8,128)} %bitcast.93), calls=%async_computation.1 | async-start | bytes 1048576 | tf_op jit(solution)/shard_map/all_to_all | solution.py:252
  90.7 14.3 %all-to-all-done.1 = f32[32,5,512]{2,1,0:T(8,128)S(1)} async-done(((f32[32,5,512]{2,1,0:T(8,128)}), f32[32,5,512]{2,1,0:T(8,128)S(1)}, u32[]{:S(2)}, u32[]{:S(2)}) %all-to-all-start.1) | async-done | bytes 327712 | tf_op jit(solution)/shard_map/all_to_all | solution.py:252
  105.0 12.2 %coast_couple.1 = f32[4,128,128]{2,1,0:T(8,128)S(1)} custom-call(f32[5,16384]{1,0:T(8,128)S(1)} %bitcast.94), custom_call_target="tpu_custom_call" | custom-call | tf_op jit(solution)/shard_map/coast_couple/pallas_call | solution.py:221
  117.3 4.6 %fusion.24 = f32[128,1,2,128]{3,1,2,0:T(1,128)S(1)} fusion(bf16[128,2,128,128]{3,2,1,0:T(8,128)(2,1)} %param.18, bf16[128,128,1,1]{1,0,2,3:T(8,128)(2,1)S(1)} %convert_bitcast_fusion.2), kind=kOutput, calls=%fused_computation.29 | convolution fusion | flops 8388608 | bytes 8552448 | tf_op jit(solution)/shard_map/bkij,bi->bkj/dot_general | solution.py:262
  122.3 12.9 %all_to_all.25 = f32[4,128,128]{2,1,0:T(8,128)S(1)} all-to-all(f32[4,128,128]{2,1,0:T(8,128)S(1)} %fusion.4), channel_id=1, replica_groups=mesh['land'=8,'sea'=4] {'sea'}, dimensions={0} | all-to-all | bytes 524288 | tf_op jit(solution)/shard_map/all_to_all | solution.py:266
  135.2 4.6 %fusion.22 = f32[128,1,2,128]{3,1,2,0:T(1,128)S(1)} fusion(bf16[128,2,128,128]{3,2,1,0:T(8,128)(2,1)} %param.18, bf16[128,128,1,1]{1,0,2,3:T(8,128)(2,1)S(1)} %get-tuple-element.6), kind=kOutput, calls=%fused_computation.27 | convolution fusion | flops 8388608 | bytes 8552448 | tf_op jit(solution)/shard_map/bkij,bi->bkj/dot_general | solution.py:262
  140.2 10.9 %all_to_all.26 = f32[4,128,128]{2,1,0:T(8,128)S(1)} all-to-all(f32[4,128,128]{2,1,0:T(8,128)S(1)} %fusion.2), channel_id=1, replica_groups=mesh['land'=8,'sea'=4] {'sea'}, dimensions={0} | all-to-all | bytes 524288 | tf_op jit(solution)/shard_map/all_to_all | solution.py:266
  151.2 4.6 %fusion.20 = f32[128,1,2,128]{3,1,2,0:T(1,128)S(1)} fusion(bf16[128,2,128,128]{3,2,1,0:T(8,128)(2,1)} %param.18, bf16[128,128,1,1]{1,0,2,3:T(8,128)(2,1)S(1)} %convert_bitcast_fusion), kind=kOutput, calls=%fused_computation.25 | convolution fusion | flops 8388608 | bytes 8552448 | tf_op jit(solution)/shard_map/bkij,bi->bkj/dot_general | solution.py:262
  156.2 11.0 %all_to_all.27 = f32[4,128,128]{2,1,0:T(8,128)S(1)} all-to-all(f32[4,128,128]{2,1,0:T(8,128)S(1)} %fusion), channel_id=1, replica_groups=mesh['land'=8,'sea'=4] {'sea'}, dimensions={0} | all-to-all | bytes 524288 | tf_op jit(solution)/shard_map/all_to_all | solution.py:266
  (56 shorter events, 14.2 us)
Async XLA Ops:
  0.6 19.9 %copy-start.7 = (f32[128,128]{1,0:T(8,128)S(1)}, f32[128,128]{1,0:T(8,128)}, u32[]{:S(2)}) copy-start(f32[128,128]{1,0:T(8,128)} %param.17) | copy-start | bytes 196612
  3.5 29.6 %copy-start = (f32[512,512]{1,0:T(8,128)S(1)}, f32[512,512]{1,0:T(8,128)}, u32[]{:S(2)}) copy-start(f32[512,512]{1,0:T(8,128)} %depth.1) | copy-start | bytes 3145732
  3.5 29.6 %copy-start.1 = (f32[512,512]{1,0:T(8,128)S(1)}, f32[512,512]{1,0:T(8,128)}, u32[]{:S(2)}) copy-start(f32[512,512]{1,0:T(8,128)} %cond.1) | copy-start | bytes 3145732
  11.8 21.3 %collective-permute-start = (f32[6,4,512]{2,1,0:T(4,128)}, f32[6,4,512]{2,1,0:T(4,128)S(1)}, u32[]{:S(2)}, u32[]{:S(2)}) collective-permute-start(f32[6,4,512]{2,1,0:T(4,128)} %maximum_bitcast_fusion), channel_id=1, source_target_pairs={{0,1},{1,2},{2,3},{4,5},{5,6},{6,7},{8,9},{9,10},{10,11},{12,13},{... | collective-permute-start | bytes 147464 | tf_op jit(solution)/shard_map/ppermute | solution.py:20
  18.3 16.5 %collective-permute-start.1 = (f32[6,4,512]{2,1,0:T(4,128)S(1)}, f32[6,4,512]{2,1,0:T(4,128)S(1)}, u32[]{:S(2)}, u32[]{:S(2)}) collective-permute-start(f32[6,4,512]{2,1,0:T(4,128)S(1)} %maximum_bitcast_fusion.1), channel_id=1, source_target_pairs={{1,0},{2,1},{3,2},{5,4},{6,5},{7,6},{9,8},{10,9},{11,10},{13,12},{... | collective-permute-start | bytes 147464 | tf_op jit(solution)/shard_map/ppermute | solution.py:20
  26.3 58.3 %all-to-all-start = ((f32[4,128,128]{2,1,0:T(8,128)}), f32[4,128,128]{2,1,0:T(8,128)S(1)}, u32[]{:S(2)}, u32[]{:S(2)}) async-start(f32[4,128,128]{2,1,0:T(8,128)} %fusion.6), calls=%async_computation | async-start | bytes 524288 | tf_op jit(solution)/shard_map/all_to_all | solution.py:266
  37.3 16.5 %copy-start.3 = (s32[8192]{0:T(1024)S(1)}, s32[8192]{0:T(1024)}, u32[]{:S(2)}) copy-start(s32[8192]{0:T(1024)} %param.13) | copy-start | bytes 98308
  37.3 16.5 %copy-start.4 = (s32[8192,1]{0,1:T(1,128)S(1)}, s32[8192,1]{0,1:T(1,128)}, u32[]{:S(2)}) copy-start(s32[8192,1]{0,1:T(1,128)} %param.14) | copy-start | bytes 98308
  37.3 16.5 %copy-start.5 = (s32[8192]{0:T(1024)S(1)}, s32[8192]{0:T(1024)}, u32[]{:S(2)}) copy-start(s32[8192]{0:T(1024)} %param.15) | copy-start | bytes 98308
  37.3 16.5 %copy-start.6 = (f32[8192]{0:T(1024)S(1)}, f32[8192]{0:T(1024)}, u32[]{:S(2)}) copy-start(f32[8192]{0:T(1024)} %param.16) | copy-start | bytes 98308
  37.4 8.0 %collective-permute-start.3 = (f32[6,4,520]{2,1,0:T(4,128)S(1)}, f32[6,4,520]{2,1,0:T(4,128)S(1)}, u32[]{:S(2)}, u32[]{:S(2)}) collective-permute-start(f32[6,4,520]{2,1,0:T(4,128)S(1)} %pad_maximum_fusion.1), channel_id=1, source_target_pairs={{4,0},{8,4},{12,8},{16,12},{20,16},{24,20},{28,24},{5,1},{9,5},{13... | collective-permute-start | bytes 149768 | tf_op jit(solution)/shard_map/ppermute | solution.py:20
  38.8 6.7 %collective-permute-start.2 = (f32[6,4,520]{2,1,0:T(4,128)S(1)}, f32[6,4,520]{2,1,0:T(4,128)S(1)}, u32[]{:S(2)}, u32[]{:S(2)}) collective-permute-start(f32[6,4,520]{2,1,0:T(4,128)S(1)} %pad_maximum_fusion), channel_id=1, source_target_pairs={{0,4},{4,8},{8,12},{12,16},{16,20},{20,24},{24,28},{1,5},{5,9},{9,... | collective-permute-start | bytes 149768 | tf_op jit(solution)/shard_map/ppermute | solution.py:20
  53.8 1.6 copy-start.2
  84.6 20.4 %all-to-all-start.1 = ((f32[32,5,512]{2,1,0:T(8,128)}), f32[32,5,512]{2,1,0:T(8,128)S(1)}, u32[]{:S(2)}, u32[]{:S(2)}) async-start(f32[32,5,512]{2,1,0:T(8,128)} %bitcast.93), calls=%async_computation.1 | async-start | bytes 1048576 | tf_op jit(solution)/shard_map/all_to_all | solution.py:252

commit v2 on v1

--- a/solution.py
+++ b/solution.py
@@ -13,37 +13,100 @@
 HALO = STEPS
 
 
-def exchanged(last, first, axis):
-    count = lax.axis_size(axis)
-    forward = [(i, i + 1) for i in range(count - 1)]
-    backward = [(target, source) for source, target in forward]
-    return lax.ppermute(last, axis, forward), lax.ppermute(first, axis, backward)
-
-
-def fields(depth, conductance, wet, rows, columns):
-    return jnp.concatenate(
-        [
-            depth[None, rows, columns],
-            conductance[None, rows, columns],
-            wet[:, rows, columns].astype(jnp.float32),
-        ],
-        axis=0,
-    )
-
-
-def land_kernel(depth, cond, wet, left, right, top, bottom, out, masked, ext):
+MESH = pl.DeviceIdType.MESH
+
+
+def beside_of(axis):
+    count, me = lax.axis_size(axis), lax.axis_index(axis)
+    return lax.rem(me + count - 1, count), lax.rem(me + 1, count)
+
+
+def land_kernel(depth, cond, wet, out, masked, ext, out_edge, in_edge, sends, recvs):
     rows, cols = depth.shape
+    total = 2 + STEPS
+    used = total * HALO
+    height, width = ext.shape[1], ext.shape[2]
     mid_r, mid_c = pl.ds(SUB, rows), pl.ds(LANES, cols)
+    west, east = beside_of("sea")
+    north, south = beside_of("land")
+
+    barrier = pltpu.get_barrier_semaphore()
+    for to in ({"sea": west}, {"sea": east}, {"land": north}, {"land": south}):
+        pl.semaphore_signal(barrier, inc=1, device_id=to, device_id_type=MESH)
+
     ext[0, mid_r, mid_c] = depth[...]
     ext[1, mid_r, mid_c] = cond[...]
     for t in range(STEPS):
         ext[2 + t, mid_r, mid_c] = wet[t].astype(jnp.float32)
-    for i in range(2 + STEPS):
-        ext[i, mid_r, pl.ds(0, LANES)] = left[i]
-        ext[i, mid_r, pl.ds(LANES + cols, LANES)] = right[i]
-        ext[i, pl.ds(0, SUB), :] = top[i]
-        ext[i, pl.ds(SUB + rows, SUB), :] = bottom[i]
-    height, width = ext.shape[1], ext.shape[2]
+
+    lane = lax.broadcasted_iota(jnp.int32, (rows, LANES), 1)
+
+    def gathered(start, first):
+        edge = jnp.zeros((rows, LANES), jnp.float32)
+        for i in range(total):
+            tile = ext[i, mid_r, pl.ds(start, LANES)]
+            shift = (i * HALO - first) % LANES
+            tile = pltpu.roll(tile, shift, 1) if shift else tile
+            edge = jnp.where(lane // HALO == i, tile, edge)
+        return edge.T[:used]
+
+    out_edge[0] = gathered(LANES, 0)
+    out_edge[1] = gathered(cols, LANES - HALO)
+    for side in range(2):
+        in_edge[side, used:, :] = jnp.zeros((LANES - used, rows), jnp.float32)
+    pl.semaphore_wait(barrier, 4)
+
+    copies = [
+        pltpu.make_async_remote_copy(
+            src_ref=out_edge.at[side],
+            dst_ref=in_edge.at[side, pl.ds(0, used)],
+            send_sem=sends.at[side],
+            recv_sem=recvs.at[side],
+            device_id={"sea": to},
+            device_id_type=MESH,
+        )
+        for side, to in ((0, west), (1, east))
+    ]
+    for copy in copies:
+        copy.start()
+    for copy in copies:
+        copy.wait()
+
+    def spread_out(side, start, first, present):
+        edge = in_edge[side].T
+        for i in range(total):
+            shift = (first - i * HALO) % LANES
+            tile = pltpu.roll(edge, shift, 1) if shift else edge
+            keep = (lane >= first) & (lane < first + HALO) & present
+            ext[i, mid_r, pl.ds(start, LANES)] = jnp.where(keep, tile, 0.0)
+
+    sea, seas = lax.axis_index("sea"), lax.axis_size("sea")
+    land, lands = lax.axis_index("land"), lax.axis_size("land")
+    spread_out(1, 0, LANES - HALO, sea > 0)
+    spread_out(0, LANES + cols, 0, sea < seas - 1)
+
+    copies = [
+        pltpu.make_async_remote_copy(
+            src_ref=ext.at[:, pl.ds(source, SUB), :],
+            dst_ref=ext.at[:, pl.ds(target, SUB), :],
+            send_sem=sends.at[slot],
+            recv_sem=recvs.at[slot],
+            device_id={"land": to},
+            device_id_type=MESH,
+        )
+        for slot, source, target, to in (
+            (2, SUB, SUB + rows, north),
+            (3, rows, 0, south),
+        )
+    ]
+    for copy in copies:
+        copy.start()
+    for copy in copies:
+        copy.wait()
+    for start, present in ((0, land > 0), (SUB + rows, land < lands - 1)):
+        strip = ext[1, pl.ds(start, SUB), :]
+        ext[1, pl.ds(start, SUB), :] = strip * jnp.where(present, 1.0, 0.0)
+
     for t in range(STEPS):
         wet_land = ext[2 + t] * ext[0]
         masked[t] = wet_land[SUB : SUB + rows, LANES : LANES + cols].astype(jnp.bfloat16)
@@ -60,40 +123,85 @@
 
 def land_steps(depth, cond, wet):
     rows, cols = depth.shape
-    every = slice(None)
-    pick = functools.partial(fields, depth, cond, wet)
-    first_c = pick(every, slice(0, HALO))
-    last_c = pick(every, slice(cols - HALO, cols))
-    left, right = exchanged(
-        last_c.transpose(0, 2, 1), first_c.transpose(0, 2, 1), "sea"
-    )
-    left, right = left.transpose(0, 2, 1), right.transpose(0, 2, 1)
-
-    def wide(where):
-        return jnp.concatenate(
-            [left[:, where], pick(where, every), right[:, where]], axis=2
-        )
-
-    top, bottom = exchanged(
-        wide(slice(rows - HALO, rows)), wide(slice(0, HALO)), "land"
-    )
-    side = LANES - HALO
-    left = jnp.pad(left, ((0, 0), (0, 0), (side, 0)))
-    right = jnp.pad(right, ((0, 0), (0, 0), (0, side)))
-    top = jnp.pad(top, ((0, 0), (SUB - HALO, 0), (side, side)))
-    bottom = jnp.pad(bottom, ((0, 0), (0, SUB - HALO), (side, side)))
+    total = 2 + STEPS
+    vmem = pl.BlockSpec(memory_space=pltpu.VMEM)
     return pl.pallas_call(
         land_kernel,
         out_shape=(
             jax.ShapeDtypeStruct((rows, cols), jnp.float32),
             jax.ShapeDtypeStruct((STEPS, rows, cols), jnp.bfloat16),
         ),
+        in_specs=[vmem] * 3,
+        out_specs=(vmem, vmem),
         scratch_shapes=[
-            pltpu.VMEM((2 + STEPS, rows + 2 * SUB, cols + 2 * LANES), jnp.float32)
+            pltpu.VMEM((total, rows + 2 * SUB, cols + 2 * LANES), jnp.float32),
+            pltpu.VMEM((2, total * HALO, rows), jnp.float32),
+            pltpu.VMEM((2, LANES, rows), jnp.float32),
+            pltpu.SemaphoreType.DMA((4,)),
+            pltpu.SemaphoreType.DMA((4,)),
         ],
-        compiler_params=pltpu.CompilerParams(vmem_limit_bytes=48 << 20),
+        compiler_params=pltpu.CompilerParams(
+            vmem_limit_bytes=40 << 20, collective_id=0, has_side_effects=True
+        ),
         name="land_steps",
-    )(depth, cond, wet, left, right, top, bottom)
+    )(depth, cond, wet)
+
+
+def share_kernel(terms, target, ocean, coupled, out, summed, got, sends, recvs):
+    group, me = lax.axis_size("sea"), lax.axis_index("sea")
+    blocks = out.shape[0]
+    others = [lax.rem(me + d, group) for d in range(1, group)]
+    barrier = pltpu.get_barrier_semaphore()
+    for to in others:
+        pl.semaphore_signal(barrier, inc=1, device_id={"sea": to}, device_id_type=MESH)
+    high, low = halves(terms[...])
+    high, low = high.astype(jnp.bfloat16), low.astype(jnp.bfloat16)
+    for s in range(group):
+        at = iota((blocks, terms.shape[0]), 0) + s * blocks
+        hot = jnp.where(at == target[...], 1.0, 0.0).astype(jnp.bfloat16)
+        summed[s] = jnp.dot(hot, high, preferred_element_type=jnp.float32) + jnp.dot(
+            hot, low, preferred_element_type=jnp.float32
+        )
+    pl.semaphore_wait(barrier, group - 1)
+    copies = [
+        pltpu.make_async_remote_copy(
+            src_ref=summed.at[to],
+            dst_ref=got.at[i],
+            send_sem=sends.at[i],
+            recv_sem=recvs.at[i],
+            device_id={"sea": to},
+            device_id_type=MESH,
+        )
+        for i, to in enumerate(others)
+    ]
+    for copy in copies:
+        copy.start()
+    result = 0.5 * ocean[...] + coupled[...] + summed[me]
+    for copy in copies:
+        copy.wait()
+    for i in range(group - 1):
+        result = result + got[i]
+    out[...] = result
+
+
+def shared_step(terms, target, ocean, coupled):
+    group = lax.axis_size("sea")
+    blocks, width = ocean.shape
+    vmem = pl.BlockSpec(memory_space=pltpu.VMEM)
+    return pl.pallas_call(
+        share_kernel,
+        out_shape=jax.ShapeDtypeStruct((blocks, width), jnp.float32),
+        in_specs=[vmem] * 4,
+        out_specs=vmem,
+        scratch_shapes=[
+            pltpu.VMEM((group, blocks, width), jnp.float32),
+            pltpu.VMEM((group - 1, blocks, width), jnp.float32),
+            pltpu.SemaphoreType.DMA((group - 1,)),
+            pltpu.SemaphoreType.DMA((group - 1,)),
+        ],
+        compiler_params=pltpu.CompilerParams(collective_id=1, has_side_effects=True),
+        name="ocean_share",
+    )(terms, target, ocean, coupled)
 
 
 def iota(shape, axis):
@@ -243,7 +351,6 @@
     ocean_target,
 ):
     devices = lax.axis_size(("land", "sea"))
-    group = lax.axis_size("sea")
     blocks = ocean_target.shape[0]
     width = adj_ocean.shape[1]
     land_out, masked = land_steps(adj_depth, conductance, wet)
@@ -252,21 +359,14 @@
     got = lax.all_to_all(packs, ("land", "sea"), split_axis=0, concat_axis=0, tiled=True)
     coupled = coupled_steps(got.transpose(1, 0, 2).reshape(STEPS + 1, -1), blocks)
 
-    target_flat = ocean_target.reshape(-1)
-    marker = (
-        target_flat[:, None] == jnp.arange(blocks * group, dtype=jnp.int32)[None, :]
-    ).astype(jnp.float32)
+    target_row = ocean_target.reshape(1, -1)
     ocean_adj = adj_ocean
     for timestep in range(STEPS):
         ocean_low = ocean_adj.astype(jnp.bfloat16)
         terms = jnp.einsum(
             "bkij,bi->bkj", ocean_blocks, ocean_low, preferred_element_type=jnp.float32
         ).reshape(-1, width)
-        summed = jnp.einsum("rc,rw->cw", marker, terms, precision=lax.Precision.HIGHEST)
-        parts = lax.all_to_all(
-            summed.reshape(group, blocks, width), "sea", split_axis=0, concat_axis=0, tiled=True
-        )
-        ocean_adj = 0.5 * ocean_adj + jnp.sum(parts, axis=0) + coupled[timestep]
+        ocean_adj = shared_step(terms, target_row, ocean_adj, coupled[timestep])
     return (land_out, ocean_adj)
 
 

time: 169 us -> 145 us (0.86)
  Pallas kernels: 48.4 us -> 95.7 us
  blocking collectives: 34.8 us -> 0 us
  starting transfers between devices: 22.7 us -> 3.62 us
  local copies, waits for them, and re-layouts: 23.3 us -> 12.7 us
  waiting for transfers between devices: 14.4 us -> 8.13 us
    pallas_call x0 -> x4, Pallas kernels: none -> 37.4 us  [shared_step(): pl.pallas_call(share_kernel, out_shape=jax.ShapeDtypeStruct((blocks, widt...]
    all_to_all x3 -> x0, blocking collectives: 34.8 us -> none  [local(): lax.all_to_all(summed.reshape(group, blocks, width), 'sea', split_axis=0,...]
    ppermute x4 -> x0, starting transfers between devices: 10.7 us -> none  [the longest x2 8.13 us: exchanged(): lax.ppermute(last, axis, forward)]
    pallas_call x1, Pallas kernels: 8.07 us -> 18 us  [land_steps(): pl.pallas_call(land_kernel, out_shape=(jax.ShapeDtypeStruct((rows, cols),...]
    slice x4 -> x0, local copies, waits for them, and re-layouts: 7.48 us -> none  [the longest x1 2.9 us: fields(): wet[:, rows, columns].astype(jnp.float32)]
    all_to_all x1, waiting for transfers between devices: 14.3 us -> 8.13 us  [local(): lax.all_to_all(packs, ('land', 'sea'), split_axis=0, concat_axis=0, tiled...]
    all_to_all x1 -> x0, starting transfers between devices: 5.93 us -> none  [local(): lax.all_to_all(summed.reshape(group, blocks, width), 'sea', split_axis=0,...]
    pad x4 -> x0, local copies, waits for them, and re-layouts: 3.59 us -> none  [the longest x1 1.88 us: land_steps(): left = jnp.pad(left, ((0, 0), (0, 0), (side, 0)))]
  transfers between devices with their start and end apart: 6 -> 1, of which waited for: 1 -> 1; matrix products, arithmetic and copies ran while one was open for 11% -> 4% of each run, Pallas kernels for 22% -> 0%
where the time goes in v2:
time: 145 us; the launch traced here: 144 us
  Pallas kernels  95.7 us (66%)
  matrix products  20.9 us (14%)
  local copies, waits for them, and re-layouts  12.7 us (9%)
  waiting for transfers between devices  8.13 us (6%)
  starting transfers between devices  3.62 us (2%)
  other arithmetic  2.54 us (2%)
    pallas_call x4, Pallas kernels, shared_step(): pl.pallas_call(share_kernel, out_shape=jax.ShapeDtypeStruct((blocks, widt...  37.4 us
    pallas_call x1, Pallas kernels, packed(): pl.pallas_call(functools.partial(send_kernel, capacity, 256), grid=(steps...  28.1 us
    dot_general x4, matrix products, local(): jnp.einsum('bkij,bi->bkj', ocean_blocks, ocean_low, preferred_element_typ...  20.9 us
    pallas_call x1, Pallas kernels, land_steps(): pl.pallas_call(land_kernel, out_shape=(jax.ShapeDtypeStruct((rows, cols),...  18 us
    pallas_call x1, Pallas kernels, coupled_steps(): pl.pallas_call(couple_kernel, grid=(slots // count,), in_specs=[pl.BlockS...  12.2 us
    unnamed x21, local copies, waits for them, and re-layouts  10.2 us
    all_to_all x1, waiting for transfers between devices, local(): lax.all_to_all(packs, ('land', 'sea'), split_axis=0, concat_axis=0, tiled...  8.13 us
    all_to_all x1, starting transfers between devices, local(): lax.all_to_all(packs, ('land', 'sea'), split_axis=0, concat_axis=0, tiled...  3.62 us
  transfers between devices with their start and end apart: 1, of which 1 were waited for; matrix products, arithmetic and copies ran while one was open for 4% of the time, Pallas kernels for 0%

profile of v2, /device:TPU:0, one launch (start us, length us, event | category | flops | bytes accessed | tf_op | source)
XLA Modules:
  0.0 144.4 jit_solution(15684795492046156091)
XLA Ops:
  0.6 2.2 %copy-done = s32[4,512,512]{2,1,0:T(8,128)S(1)} copy-done((s32[4,512,512]{2,1,0:T(8,128)S(1)}, s32[4,512,512]{2,1,0:T(8,128)}, u32[]{:S(2)}) %copy-start) | copy-done | bytes 4194328
  2.8 1.2 copy-done.1
  4.0 1.2 copy-done.2
  5.3 18.0 %land_steps.1 = (f32[512,512]{1,0:T(8,128)S(1)}, bf16[4,512,512]{2,1,0:T(8,128)(2,1)S(1)}) custom-call(f32[512,512]{1,0:T(8,128)S(1)} %copy-done.1, f32[512,512]{1,0:T(8,128)S(1)} %copy-done.2, s32[4,512,512]{2,1,0:T(8,128)S(1)} %copy-done), custom_call_target="tpu_custom_call" | custom-call | tf_op jit(solution)/shard_map/land_steps/pallas_call | solution.py:128
  24.0 0.8 copy-done.4
  24.8 0.8 copy-done.5
  26.3 28.1 %coast_pack.1 = f32[5,128,128]{2,1,0:T(8,128)S(1)} custom-call(s32[8,1,1024]{2,1,0:T(1,128)S(1)} %bitcast.47, s32[8,1,1024]{2,1,0:T(1,128)S(1)} %bitcast.48, s32[8,1,1024]{2,1,0:T(1,128)S(1)} %bitcast.49, f32[8,1,1024]{2,1,0:T(1,128)S(1)} %bitcast.50, bf16[4,512,512]{2,1,0:T(8,128)(2,1)S(1)} %get-tuple-element.5.masked), custom_call_target="tpu_custom_call" | custom-call | tf_op jit(solution)/shard_map/coast_pack/pallas_call | solution.py:291
  54.5 1.0 copy.33
  55.5 3.6 %all-to-all-start = ((f32[32,5,512]{2,1,0:T(8,128)}), f32[32,5,512]{2,1,0:T(8,128)S(1)}, u32[]{:S(2)}, u32[]{:S(2)}) async-start(f32[32,5,512]{2,1,0:T(8,128)} %bitcast.45), calls=%async_computation | async-start | bytes 1048576 | tf_op jit(solution)/shard_map/all_to_all | solution.py:359
  59.9 5.2 %fusion.6 = f32[128,1,2,128]{3,1,2,0:T(1,128)} fusion(bf16[128,2,128,128]{3,2,1,0:T(8,128)(2,1)} %param.18, bf16[128,128,1,1]{1,0,2,3:T(8,128)(2,1)S(1)} %convert_bitcast_fusion.3), kind=kOutput, calls=%fused_computation.11 | convolution fusion | flops 8388608 | bytes 8552448 | tf_op jit(solution)/shard_map/bkij,bi->bkj/dot_general | solution.py:366
  65.1 8.1 %all-to-all-done = f32[32,5,512]{2,1,0:T(8,128)S(1)} async-done(((f32[32,5,512]{2,1,0:T(8,128)}), f32[32,5,512]{2,1,0:T(8,128)S(1)}, u32[]{:S(2)}, u32[]{:S(2)}) %all-to-all-start) | async-done | bytes 327712 | tf_op jit(solution)/shard_map/all_to_all | solution.py:359
  73.3 12.2 %coast_couple.1 = f32[4,128,128]{2,1,0:T(8,128)S(1)} custom-call(f32[5,16384]{1,0:T(8,128)S(1)} %bitcast.46), custom_call_target="tpu_custom_call" | custom-call | tf_op jit(solution)/shard_map/coast_couple/pallas_call | solution.py:329
  86.2 11.2 %ocean_share.4.ocean = f32[128,128]{1,0:T(8,128)} custom-call(f32[256,128]{1,0:T(8,128)} %bitcast.54, s32[1,256]{1,0:T(1,128)} %reshape.38.target, f32[128,128]{1,0:T(8,128)} %ocean.1, f32[128,128]{1,0:T(8,128)} %get-tuple-element.9.coupled), custom_call_target="tpu_custom_call" | custom-call | tf_op jit(solution)/shard_map/ocean_share/pallas_call | solution.py:191
  97.4 0.8 convert_bitcast_fusion.2
  98.3 5.2 %fusion.4 = f32[128,1,2,128]{3,1,2,0:T(1,128)} fusion(bf16[128,2,128,128]{3,2,1,0:T(8,128)(2,1)} %param.18, bf16[128,128,1,1]{1,0,2,3:T(8,128)(2,1)S(1)} %convert_bitcast_fusion.2), kind=kOutput, calls=%fused_computation.9 | convolution fusion | flops 8388608 | bytes 8552448 | tf_op jit(solution)/shard_map/bkij,bi->bkj/dot_general | solution.py:366
  103.5 8.8 %ocean_share.5.ocean = f32[128,128]{1,0:T(8,128)} custom-call(f32[256,128]{1,0:T(8,128)} %bitcast.52, s32[1,256]{1,0:T(1,128)} %reshape.38.target, f32[128,128]{1,0:T(8,128)} %ocean_share.4.ocean, f32[128,128]{1,0:T(8,128)} %get-tuple-element.8.coupled), custom_call_target="tpu_custom_call" | custom-call | tf_op jit(solution)/shard_map/ocean_share/pallas_call | solution.py:191
  112.3 0.8 convert_bitcast_fusion.1
  113.2 5.2 %fusion.2 = f32[128,1,2,128]{3,1,2,0:T(1,128)} fusion(bf16[128,2,128,128]{3,2,1,0:T(8,128)(2,1)} %param.18, bf16[128,128,1,1]{1,0,2,3:T(8,128)(2,1)S(1)} %convert_bitcast_fusion.1), kind=kOutput, calls=%fused_computation.7 | convolution fusion | flops 8388608 | bytes 8552448 | tf_op jit(solution)/shard_map/bkij,bi->bkj/dot_general | solution.py:366
  118.4 8.3 %ocean_share.6.ocean = f32[128,128]{1,0:T(8,128)} custom-call(f32[256,128]{1,0:T(8,128)} %bitcast.53, s32[1,256]{1,0:T(1,128)} %reshape.38.target, f32[128,128]{1,0:T(8,128)} %ocean_share.5.ocean, f32[128,128]{1,0:T(8,128)} %get-tuple-element.7.coupled), custom_call_target="tpu_custom_call" | custom-call | tf_op jit(solution)/shard_map/ocean_share/pallas_call | solution.py:191
  126.7 0.8 convert_bitcast_fusion
  127.6 5.2 %fusion = f32[128,1,2,128]{3,1,2,0:T(1,128)} fusion(bf16[128,2,128,128]{3,2,1,0:T(8,128)(2,1)} %param.18, bf16[128,128,1,1]{1,0,2,3:T(8,128)(2,1)S(1)} %convert_bitcast_fusion), kind=kOutput, calls=%fused_computation.5 | convolution fusion | flops 8388608 | bytes 8552448 | tf_op jit(solution)/shard_map/bkij,bi->bkj/dot_general | solution.py:366
  132.8 9.1 %ocean_share.7 = f32[128,128]{1,0:T(8,128)} custom-call(f32[256,128]{1,0:T(8,128)} %bitcast.51, s32[1,256]{1,0:T(1,128)} %reshape.38.target, f32[128,128]{1,0:T(8,128)} %ocean_share.6.ocean, f32[128,128]{1,0:T(8,128)} %get-tuple-element.6.coupled), custom_call_target="tpu_custom_call" | custom-call | tf_op jit(solution)/shard_map/ocean_share/pallas_call | solution.py:191
  141.9 1.0 copy.36
  142.9 1.5 %copy.37 = f32[128,128]{1,0:T(8,128)} copy(f32[128,128]{1,0:T(8,128)} %ocean_share.7) | data formatting | bytes 131072
  (18 shorter events, 3.1 us)
Async XLA Ops:
  0.6 2.2 %copy-start = (s32[4,512,512]{2,1,0:T(8,128)S(1)}, s32[4,512,512]{2,1,0:T(8,128)}, u32[]{:S(2)}) copy-start(s32[4,512,512]{2,1,0:T(8,128)} %wet.1) | copy-start | bytes 12582916
  2.8 1.2 copy-start.1
  4.0 1.2 copy-start.2
  5.3 53.8 %copy-start.7 = (f32[128,128]{1,0:T(8,128)S(1)}, f32[128,128]{1,0:T(8,128)}, u32[]{:S(2)}) copy-start(f32[128,128]{1,0:T(8,128)} %ocean.1) | copy-start | bytes 196612
  5.3 53.8 %copy-start.8 = (s32[128,2]{0,1:T(2,128)S(1)}, s32[128,2]{0,1:T(2,128)}, u32[]{:S(2)}) copy-start(s32[128,2]{0,1:T(2,128)} %param.19) | copy-start | bytes 3076
  23.2 0.8 copy-start.3
  24.0 0.8 copy-start.4
  24.8 0.8 copy-start.5
  25.5 0.8 copy-start.6
  55.5 17.8 %all-to-all-start = ((f32[32,5,512]{2,1,0:T(8,128)}), f32[32,5,512]{2,1,0:T(8,128)S(1)}, u32[]{:S(2)}, u32[]{:S(2)}) async-start(f32[32,5,512]{2,1,0:T(8,128)} %bitcast.45), calls=%async_computation | async-start | bytes 1048576 | tf_op jit(solution)/shard_map/all_to_all | solution.py:359
